TPU v7x, 256 devices: a whole 4x4x8 slice. The times are simulated.
256 devices in a mesh: dp: 32 (over y, z), tensor: 8 (over x, core).
Axes of the slice: x: 4, y: 4, z: 8, core: 2. Of those that a mesh axis runs over, the one named last changes fastest.
Arguments:
- queries: bfloat16 [256, 6, 8192], P('dp', None, 'tensor'), may hold values from -150 to 150
- new_keys: bfloat16 [256, 6, 1024], P('dp', None, 'tensor'), may hold values from -6 to 6
- new_values: bfloat16 [256, 6, 1024], P('dp', None, 'tensor'), may hold values from -6 to 6
- key_cache: bfloat16 [256, 256, 1024], P('dp', None, 'tensor'), may hold values from -6 to 6
- value_cache: bfloat16 [256, 256, 1024], P('dp', None, 'tensor'), may hold values from -6 to 6
- cache_lengths: int32 [256], P('dp'), may hold values from 32 to 256, as said below
- accepted: int32 [256], P('tensor'), may hold values from 1 to 6
- residual: bfloat16 [256, 6, 8192], P('tensor', None, 'dp'), may hold values from -6 to 6
- out_weight: bfloat16 [8192, 8192], P('tensor', 'dp'), may hold values from -0.0625 to 0.0625
- draft_weight: bfloat16 [8192, 8192], P('tensor', 'dp'), may hold values from -0.0625 to 0.0625
Outputs:
- verified: bfloat16 [256, 6, 8192], P('tensor', None, 'dp')
- drafted: bfloat16 [5, 256, 8192], P(None, 'tensor', 'dp')
Inputs may be any that keep to these rules, and one draw needn't show every extreme that they name: `cache_lengths`: every draw has a window with all 256 slots live.
All inputs are finite; a program needn't handle non-finite values.
Results may differ from a plain program's by a relative error of at most 0.008.
Values may be sent and summed in bfloat16 or wider, within the bound.
No kernel may reach another device: no remote copies, remote signals or barrier semaphores. Data moves between devices by JAX's collectives and lax.ppermute only.
A program may use at most 64 MiB of HBM per device.

v0:
```python
import jax
import jax.numpy as jnp
from jax import lax
from jax.sharding import PartitionSpec as P

HD = 128
STEPS = 5


def widen(drafted_rows):
    wide_rows = lax.all_gather(drafted_rows, "dp", axis=1, tiled=True)
    return lax.all_to_all(wide_rows, "tensor", split_axis=1, concat_axis=0, tiled=True)


def per_device(
    queries,
    new_keys,
    new_values,
    key_cache,
    value_cache,
    cache_lengths,
    accepted,
    residual,
    out_weight,
    draft_weight,
):
    windows_here, tokens_here, query_width = queries.shape
    cache_size = key_cache.shape[1]
    kv_here = new_keys.shape[2] // HD
    group_size = query_width // HD // kv_here
    query_split = queries.reshape(windows_here, tokens_here, kv_here, group_size, HD)
    keys_cached = key_cache.reshape(windows_here, cache_size, kv_here, HD)
    keys_fresh = new_keys.reshape(windows_here, tokens_here, kv_here, HD)
    score_cache = jnp.einsum(
        "wtkgd,wpkd->wkgtp", query_split, keys_cached, preferred_element_type=jnp.float32
    ) * HD ** (-0.5)
    score_fresh = jnp.einsum(
        "wtkgd,wpkd->wkgtp", query_split, keys_fresh, preferred_element_type=jnp.float32
    ) * HD ** (-0.5)
    live_cache = (jnp.arange(cache_size)[None, :] < cache_lengths[:, None])[:, None, None, None, :]
    live_fresh = jnp.arange(tokens_here)[None, :] <= jnp.arange(tokens_here)[:, None]
    scores = jnp.concatenate(
        [
            jnp.where(live_cache, score_cache, -jnp.inf),
            jnp.where(live_fresh, score_fresh, -jnp.inf),
        ],
        axis=-1,
    )
    largest = jnp.max(scores, axis=-1, keepdims=True)
    powered = jnp.exp(scores - largest)
    weights = (powered / jnp.sum(powered, axis=-1, keepdims=True)).astype(jnp.bfloat16)
    values_cached = value_cache.reshape(windows_here, cache_size, kv_here, HD)
    values_fresh = new_values.reshape(windows_here, tokens_here, kv_here, HD)
    mixed_rows = jnp.einsum(
        "wkgtp,wpkd->wtkgd",
        weights[..., :cache_size],
        values_cached,
        preferred_element_type=jnp.float32,
    )
    mixed_rows = mixed_rows + jnp.einsum(
        "wkgtp,wpkd->wtkgd",
        weights[..., cache_size:],
        values_fresh,
        preferred_element_type=jnp.float32,
    )
    attended = mixed_rows.astype(jnp.bfloat16).reshape(windows_here * tokens_here, query_width)
    partial_out = jnp.dot(
        lax.all_gather(attended, "dp", axis=0, tiled=True),
        out_weight,
        preferred_element_type=jnp.float32,
    )
    summed = lax.psum_scatter(partial_out, "tensor", scatter_dimension=0, tiled=True)
    block_windows, block_tokens, block_cols = residual.shape
    flat_residual = residual.reshape(block_windows * block_tokens, block_cols).astype(jnp.float32)
    verified = (
        (flat_residual + summed)
        .astype(jnp.bfloat16)
        .reshape(block_windows, block_tokens, block_cols)
    )
    chosen = jnp.arange(block_tokens)[None, :] == (accepted - 1)[:, None]
    picked = jnp.sum(
        jnp.where(chosen[:, :, None], verified, jnp.zeros((), jnp.bfloat16)),
        axis=1,
        dtype=jnp.bfloat16,
    )
    results = []
    current = widen(picked)
    row_block = current.shape[0] // lax.axis_size("tensor")
    row_start = lax.axis_index("tensor") * row_block
    for draft_step in range(STEPS):
        everyone = lax.psum(
            jnp.dot(current, draft_weight, preferred_element_type=jnp.float32), "tensor"
        )
        share = lax.dynamic_slice_in_dim(everyone, row_start, row_block, 0)
        drafted_now = jnp.tanh(2.0 * share).astype(jnp.bfloat16)
        results.append(drafted_now)
        if draft_step + 1 < STEPS:
            current = widen(drafted_now)
    return (verified, jnp.stack(results))


def solution(mesh):
    placed = (
        P("dp", None, "tensor"),
        P("dp", None, "tensor"),
        P("dp", None, "tensor"),
        P("dp", None, "tensor"),
        P("dp", None, "tensor"),
        P("dp"),
        P("tensor"),
        P("tensor", None, "dp"),
        P("tensor", "dp"),
        P("tensor", "dp"),
    )
    return jax.shard_map(
        per_device,
        mesh=mesh,
        in_specs=placed,
        out_specs=(P("tensor", None, "dp"), P(None, "tensor", "dp")),
        check_vma=False,
    )
```

profile of v0, /device:TPU:8, one launch (start us, length us, event | category | flops | bytes accessed | tf_op | source)
XLA Modules:
  0.0 744.6 jit_solution(10365520250779408295)
XLA Ops:
  7.2 0.0 copy-start
  7.2 0.0 copy-start.2
  7.2 0.0 all-gather.2.cloned.1.call-start
  7.2 0.8 iota_compare_fusion.1
  8.1 1.4 fusion.17
  9.5 1.2 fusion.18
  10.7 0.3 fusion.9
  11.0 0.2 divide_convert_fusion
  11.1 0.9 fusion.10
  12.0 0.0 copy-done.2
  12.0 0.2 fusion.4
  12.2 0.7 copy.94
  12.9 0.0 all-gather.2.cloned.1.call-update
  12.9 0.0 copy-start.3
  12.9 0.0 copy-start.5
  12.9 0.0 reduce-scatter.2.cloned.1.call-start
  13.0 81.7 %all-gather.2.cloned.1.call-done = bf16[1536,1024]{1,0:T(8,128)(2,1)} async-done(((bf16[48,1024]{1,0:T(8,128)(2,1)}), bf16[1536,1024]{1,0:T(8,128)(2,1)}) %all-gather.2.cloned.1.call-update) | async-done | bytes 3145744 | tf_op jit(solution)/shard_map/all_gather | solution.py:68
  94.7 4.0 fusion.19
  98.7 0.0 reduce-scatter.2.cloned.1.call-update
  98.7 0.0 all-reduce.6.cloned.1.call-start
  98.8 0.0 copy-done.3
  98.8 0.1 copy.42
  98.9 0.0 copy-done.5
  98.9 0.1 iota_compare_fusion
  99.0 32.9 %reduce-scatter.2.cloned.1.call-done = f32[192,256]{1,0:T(8,128)} async-done(((f32[1536,256]{1,0:T(8,128)}), f32[192,256]{1,0:T(8,128)}) %reduce-scatter.2.cloned.1.call-update) | async-done | bytes 196624 | tf_op jit(solution)/shard_map/reduce_scatter | solution.py:72
  131.9 0.9 add_convert_fusion
  132.9 0.1 select_reduce_fusion
  133.0 43.9 %all_gather.19 = bf16[32,8192]{1,0:T(8,128)(2,1)S(1)} all-gather(bf16[32,256]{1,0:T(8,128)(2,1)S(1)} %select_reduce_fusion), channel_id=1, replica_groups=mesh['dp'=32,'tensor'=8] {'dp'}, dimensions={1}, use_global_device_ids=true | all-gather | bytes 540672 | tf_op jit(solution)/shard_map/all_gather | solution.py:11
  177.0 12.8 %all_to_all.95 = bf16[32,8,1024]{2,0,1:T(8,128)(2,1)S(1)} all-to-all(bf16[32,8,1024]{2,0,1:T(8,128)(2,1)S(1)} %bitcast.106), channel_id=1, replica_groups=mesh['dp'=32,'tensor'=8] {'tensor'}, dimensions={1} | all-to-all | bytes 1048576 | tf_op jit(solution)/shard_map/all_to_all | solution.py:12
  189.8 1.0 fusion.20
  190.8 0.0 all-reduce.6.cloned.1.call-update
  190.8 0.0 all-reduce.8.cloned.1.call-start
  190.9 62.3 %all-reduce.6.cloned.1.call-done = f32[256,256]{1,0:T(8,128)} async-done(((f32[256,256]{1,0:T(8,128)}), f32[256,256]{1,0:T(8,128)}) %all-reduce.6.cloned.1.call-update) | async-done | bytes 262160 | tf_op jit(solution)/shard_map/psum | solution.py:91
  253.1 0.8 bitcast_dynamic-update-slice_fusion.3
  253.9 43.9 %all_gather.20 = bf16[32,8192]{1,0:T(8,128)(2,1)S(1)} all-gather(bf16[32,256]{1,0:T(8,128)(2,1)S(1)} %get-tuple-element.17), channel_id=1, replica_groups=mesh['dp'=32,'tensor'=8] {'dp'}, dimensions={1}, use_global_device_ids=true | all-gather | bytes 540672 | tf_op jit(solution)/shard_map/all_gather | solution.py:11
  297.8 12.8 %all_to_all.96 = bf16[32,8,1024]{2,0,1:T(8,128)(2,1)S(1)} all-to-all(bf16[32,8,1024]{2,0,1:T(8,128)(2,1)S(1)} %bitcast.109), channel_id=1, replica_groups=mesh['dp'=32,'tensor'=8] {'tensor'}, dimensions={1} | all-to-all | bytes 1048576 | tf_op jit(solution)/shard_map/all_to_all | solution.py:12
  310.7 1.0 fusion.21
  311.6 0.0 all-reduce.8.cloned.1.call-update
  311.7 0.0 all-reduce.10.cloned.1.call-start
  311.7 62.2 %all-reduce.8.cloned.1.call-done = f32[256,256]{1,0:T(8,128)} async-done(((f32[256,256]{1,0:T(8,128)}), f32[256,256]{1,0:T(8,128)}) %all-reduce.8.cloned.1.call-update) | async-done | bytes 262160 | tf_op jit(solution)/shard_map/psum | solution.py:91
  373.9 0.8 bitcast_dynamic-update-slice_fusion.2
  374.7 43.9 %all_gather.21 = bf16[32,8192]{1,0:T(8,128)(2,1)S(1)} all-gather(bf16[32,256]{1,0:T(8,128)(2,1)S(1)} %get-tuple-element.15), channel_id=1, replica_groups=mesh['dp'=32,'tensor'=8] {'dp'}, dimensions={1}, use_global_device_ids=true | all-gather | bytes 540672 | tf_op jit(solution)/shard_map/all_gather | solution.py:11
  418.6 12.8 %all_to_all.97 = bf16[32,8,1024]{2,0,1:T(8,128)(2,1)S(1)} all-to-all(bf16[32,8,1024]{2,0,1:T(8,128)(2,1)S(1)} %bitcast.112), channel_id=1, replica_groups=mesh['dp'=32,'tensor'=8] {'tensor'}, dimensions={1} | all-to-all | bytes 1048576 | tf_op jit(solution)/shard_map/all_to_all | solution.py:12
  431.5 1.0 fusion.22
  432.4 0.0 all-reduce.10.cloned.1.call-update
  432.5 0.0 all-reduce.12.cloned.1.call-start
  432.5 62.2 %all-reduce.10.cloned.1.call-done = f32[256,256]{1,0:T(8,128)} async-done(((f32[256,256]{1,0:T(8,128)}), f32[256,256]{1,0:T(8,128)}) %all-reduce.10.cloned.1.call-update) | async-done | bytes 262160 | tf_op jit(solution)/shard_map/psum | solution.py:91
  494.7 0.8 bitcast_dynamic-update-slice_fusion.1
  495.5 43.9 %all_gather.22 = bf16[32,8192]{1,0:T(8,128)(2,1)S(1)} all-gather(bf16[32,256]{1,0:T(8,128)(2,1)S(1)} %get-tuple-element.13), channel_id=1, replica_groups=mesh['dp'=32,'tensor'=8] {'dp'}, dimensions={1}, use_global_device_ids=true | all-gather | bytes 540672 | tf_op jit(solution)/shard_map/all_gather | solution.py:11
  539.5 12.8 %all_to_all.98 = bf16[32,8,1024]{2,0,1:T(8,128)(2,1)S(1)} all-to-all(bf16[32,8,1024]{2,0,1:T(8,128)(2,1)S(1)} %bitcast.115), channel_id=1, replica_groups=mesh['dp'=32,'tensor'=8] {'tensor'}, dimensions={1} | all-to-all | bytes 1048576 | tf_op jit(solution)/shard_map/all_to_all | solution.py:12
  552.3 1.0 fusion.23
  553.3 0.0 all-reduce.12.cloned.1.call-update
  553.3 0.0 all-reduce.14.cloned.1.call-start
  553.3 62.2 %all-reduce.12.cloned.1.call-done = f32[256,256]{1,0:T(8,128)} async-done(((f32[256,256]{1,0:T(8,128)}), f32[256,256]{1,0:T(8,128)}) %all-reduce.12.cloned.1.call-update) | async-done | bytes 262160 | tf_op jit(solution)/shard_map/psum | solution.py:91
  615.5 0.8 bitcast_dynamic-update-slice_fusion
  616.3 43.9 %all_gather.23 = bf16[32,8192]{1,0:T(8,128)(2,1)S(1)} all-gather(bf16[32,256]{1,0:T(8,128)(2,1)S(1)} %get-tuple-element.11), channel_id=1, replica_groups=mesh['dp'=32,'tensor'=8] {'dp'}, dimensions={1}, use_global_device_ids=true | all-gather | bytes 540672 | tf_op jit(solution)/shard_map/all_gather | solution.py:11
  660.3 12.8 %all_to_all.99 = bf16[32,8,1024]{2,0,1:T(8,128)(2,1)S(1)} all-to-all(bf16[32,8,1024]{2,0,1:T(8,128)(2,1)S(1)} %bitcast.118), channel_id=1, replica_groups=mesh['dp'=32,'tensor'=8] {'tensor'}, dimensions={1} | all-to-all | bytes 1048576 | tf_op jit(solution)/shard_map/all_to_all | solution.py:12
  673.1 1.0 fusion.24
  674.1 0.0 all-reduce.14.cloned.1.call-update
  674.1 0.7 copy.53
  674.8 61.6 %all-reduce.14.cloned.1.call-done = f32[256,256]{1,0:T(8,128)} async-done(((f32[256,256]{1,0:T(8,128)}), f32[256,256]{1,0:T(8,128)}) %all-reduce.14.cloned.1.call-update) | async-done | bytes 262160 | tf_op jit(solution)/shard_map/psum | solution.py:91
  736.4 0.8 fusion.14
  737.1 0.0 copy-start.4
  737.2 0.6 copy-done.4
  (13 shorter events, 0.3 us)
Async XLA Ops:
  7.2 87.5 %copy-start = (bf16[1024,256]{1,0:T(8,128)(2,1)S(1)}, bf16[1024,256]{1,0:T(8,128)(2,1)}, u32[]{:S(2)}) copy-start(bf16[1024,256]{1,0:T(8,128)(2,1)} %param.18) | copy-start | bytes 1572868
  7.2 4.8 copy-start.2
  7.2 87.5 %all-gather.2.cloned.1.call-start = ((), (), s32[]{:S(2)}) async-start(), calls=%async_computation.6 | async-start | bytes 3244032 | tf_op jit(solution)/shard_map/all_gather | solution.py:68
  12.9 85.8 %copy-start.3 = (bf16[32,6,256]{2,0,1:T(8,128)(2,1)S(1)}, bf16[32,6,256]{2,0,1:T(8,128)(2,1)}, u32[]{:S(2)}) copy-start(bf16[32,6,256]{2,0,1:T(8,128)(2,1)} %param.17) | copy-start | bytes 294916
  12.9 86.0 %copy-start.5 = (s32[32]{0:T(128)S(1)}, s32[32]{0:T(128)}, u32[]{:S(2)}) copy-start(s32[32]{0:T(128)} %param.16) | copy-start | bytes 388
  12.9 118.9 %reduce-scatter.2.cloned.1.call-start = ((), (), s32[]{:S(2)}) async-start(), calls=%async_computation.7 | async-start | bytes 1769472 | tf_op jit(solution)/shard_map/reduce_scatter | solution.py:72
  98.7 91.1 %copy-start.1 = (bf16[1024,256]{1,0:T(8,128)(2,1)S(1)}, bf16[1024,256]{1,0:T(8,128)(2,1)}, u32[]{:S(2)}) copy-start(bf16[1024,256]{1,0:T(8,128)(2,1)} %param.19) | copy-start | bytes 1572868
  98.7 154.4 %all-reduce.6.cloned.1.call-start = ((), (), s32[]{:S(2)}) async-start(), calls=%async_computation.8 | async-start | bytes 524288 | tf_op jit(solution)/shard_map/psum | solution.py:91
  190.8 183.1 %all-reduce.8.cloned.1.call-start = ((), (), s32[]{:S(2)}) async-start(), calls=%async_computation.9 | async-start | bytes 524288 | tf_op jit(solution)/shard_map/psum | solution.py:91
  311.7 183.1 %all-reduce.10.cloned.1.call-start = ((), (), s32[]{:S(2)}) async-start(), calls=%async_computation.10 | async-start | bytes 524288 | tf_op jit(solution)/shard_map/psum | solution.py:91
  432.5 183.1 %all-reduce.12.cloned.1.call-start = ((), (), s32[]{:S(2)}) async-start(), calls=%async_computation.11 | async-start | bytes 524288 | tf_op jit(solution)/shard_map/psum | solution.py:91
  553.3 183.1 %all-reduce.14.cloned.1.call-start = ((), (), s32[]{:S(2)}) async-start(), calls=%async_computation.12 | async-start | bytes 524288 | tf_op jit(solution)/shard_map/psum | solution.py:91
  737.1 0.6 copy-start.4
Sparse Core Ops, SparseCore 0:
  13.0 81.5 all-gather.1
  98.8 32.9 reduce-scatter.1
  190.9 62.1 all-reduce.5
  311.8 62.0 all-reduce.7
  432.6 62.1 all-reduce.9
  553.4 62.0 all-reduce.11
  674.2 62.1 all-reduce.13
where the time goes:
time: 745 us
  waiting for transfers between devices  425 us (57%)
  blocking collectives  284 us (38%)
  between operations  14.3 us (2%)
  matrix products  12.6 us (2%)
    psum x5, waiting for transfers between devices, per_device(): lax.psum(jnp.dot(current, draft_weight, preferred_element_type=jnp.float3...  311 us
    all_gather x5, blocking collectives, widen(): wide_rows = lax.all_gather(drafted_rows, 'dp', axis=1, tiled=True)  220 us
    all_gather x1, waiting for transfers between devices, per_device(): lax.all_gather(attended, 'dp', axis=0, tiled=True)  81.7 us
    all_to_all x5, blocking collectives, widen(): lax.all_to_all(wide_rows, 'tensor', split_axis=1, concat_axis=0, tiled=True)  64 us
    reduce_scatter x1, waiting for transfers between devices, per_device(): lax.psum_scatter(partial_out, 'tensor', scatter_dimension=0, tiled=True)  32.9 us
  transfers between devices with their start and end apart: 7, of which 7 were waited for; matrix products, arithmetic and copies ran while one was open for 0% of the time, Pallas kernels for 0%

commit v1 on v0

--- a/solution.py
+++ b/solution.py
@@ -8,7 +8,9 @@
 
 
 def widen(drafted_rows):
-    wide_rows = lax.all_gather(drafted_rows, "dp", axis=1, tiled=True)
+    wide_rows = jnp.concatenate(
+        lax.all_to_all(jnp.stack([drafted_rows] * lax.axis_size("dp")), "dp", 0, 0), axis=1
+    )
     return lax.all_to_all(wide_rows, "tensor", split_axis=1, concat_axis=0, tiled=True)
 
 

time: 745 us -> 653 us (0.88)
  blocking collectives: 284 us -> 190 us
    all_gather x5 -> x0, blocking collectives: 220 us -> none  [widen(): wide_rows = lax.all_gather(drafted_rows, 'dp', axis=1, tiled=True)]
    all_to_all x0 -> x5, blocking collectives: none -> 117 us  [widen(): lax.all_to_all(jnp.stack([drafted_rows] * lax.axis_size('dp')), 'dp', 0, 0)]
    all_to_all x5, blocking collectives: 64 us -> 73.7 us  [widen(): lax.all_to_all(wide_rows, 'tensor', split_axis=1, concat_axis=0, tiled=True)]
where the time goes in v1:
time: 653 us; the launch traced here: 652 us
  waiting for transfers between devices  421 us (64%)
  blocking collectives  190 us (29%)
  between operations  14.4 us (2%)
  matrix products  12.6 us (2%)
  local copies, waits for them, and re-layouts  6.88 us (1%)
    psum x5, waiting for transfers between devices, per_device(): lax.psum(jnp.dot(current, draft_weight, preferred_element_type=jnp.float3...  306 us
    all_to_all x5, blocking collectives, widen(): lax.all_to_all(jnp.stack([drafted_rows] * lax.axis_size('dp')), 'dp', 0, 0)  117 us
    all_gather x1, waiting for transfers between devices, per_device(): lax.all_gather(attended, 'dp', axis=0, tiled=True)  81.7 us
    all_to_all x5, blocking collectives, widen(): lax.all_to_all(wide_rows, 'tensor', split_axis=1, concat_axis=0, tiled=True)  73.7 us
    reduce_scatter x1, waiting for transfers between devices, per_device(): lax.psum_scatter(partial_out, 'tensor', scatter_dimension=0, tiled=True)  32.9 us
  transfers between devices with their start and end apart: 7, of which 7 were waited for; matrix products, arithmetic and copies ran while one was open for 0% of the time, Pallas kernels for 0%

profile of v1, /device:TPU:8, one launch (start us, length us, event | category | flops | bytes accessed | tf_op | source)
XLA Modules:
  0.0 651.8 jit_solution(4109693385243947342)
XLA Ops:
  7.2 0.8 iota_compare_fusion.1
  8.1 1.4 fusion.17
  9.5 1.2 fusion.18
  10.7 0.3 fusion.9
  11.0 0.2 divide_convert_fusion
  11.1 0.9 fusion.10
  12.0 0.2 fusion.4
  12.2 0.7 copy.73
  13.0 81.7 %all-gather.2.cloned.1.call-done = bf16[1536,1024]{1,0:T(8,128)(2,1)} async-done(((bf16[48,1024]{1,0:T(8,128)(2,1)}), bf16[1536,1024]{1,0:T(8,128)(2,1)}) %all-gather.2.cloned.1.call-update) | async-done | bytes 3145744 | tf_op jit(solution)/shard_map/all_gather | solution.py:70
  94.7 4.0 fusion.19
  98.7 0.0 all-reduce.6.cloned.1.call-start
  98.8 0.1 copy.31
  98.9 0.1 iota_compare_fusion
  99.0 32.9 %reduce-scatter.2.cloned.1.call-done = f32[192,256]{1,0:T(8,128)} async-done(((f32[1536,256]{1,0:T(8,128)}), f32[192,256]{1,0:T(8,128)}) %reduce-scatter.2.cloned.1.call-update) | async-done | bytes 196624 | tf_op jit(solution)/shard_map/reduce_scatter | solution.py:74
  131.9 0.9 add_convert_fusion
  132.9 0.1 select_reduce_fusion
  133.1 0.1 stack.22
  133.1 22.9 %all_to_all.120 = bf16[32,32,256]{2,1,0:T(8,128)(2,1)S(1)} all-to-all(bf16[32,32,256]{2,1,0:T(8,128)(2,1)S(1)} %stack.22), channel_id=1, replica_groups=mesh['dp'=32,'tensor'=8] {'dp'}, dimensions={0} | all-to-all | bytes 1048576 | tf_op jit(solution)/shard_map/all_to_all | solution.py:12
  156.0 0.3 copy.37
  156.3 0.3 all_to_all.86
  156.6 0.3 copy.38
  156.9 13.9 %all_to_all.121 = bf16[32,8,1024]{2,0,1:T(8,128)(2,1)S(1)} all-to-all(bf16[32,8,1024]{2,0,1:T(8,128)(2,1)S(1)} %copy.38), channel_id=1, replica_groups=mesh['dp'=32,'tensor'=8] {'tensor'}, dimensions={1} | all-to-all | bytes 1048576 | tf_op jit(solution)/shard_map/all_to_all | solution.py:14
  170.9 1.0 fusion.20
  171.9 62.2 %all-reduce.6.cloned.1.call-done = f32[256,256]{1,0:T(8,128)} async-done(((f32[256,256]{1,0:T(8,128)}), f32[256,256]{1,0:T(8,128)}) %all-reduce.6.cloned.1.call-update) | async-done | bytes 262160 | tf_op jit(solution)/shard_map/psum | solution.py:93
  234.1 0.8 bitcast_dynamic-update-slice_fusion.3
  234.9 0.1 stack.24
  234.9 23.4 %all_to_all.122 = bf16[32,32,256]{2,1,0:T(8,128)(2,1)S(1)} all-to-all(bf16[32,32,256]{2,1,0:T(8,128)(2,1)S(1)} %stack.24), channel_id=1, replica_groups=mesh['dp'=32,'tensor'=8] {'dp'}, dimensions={0} | all-to-all | bytes 1048576 | tf_op jit(solution)/shard_map/all_to_all | solution.py:12
  258.4 0.3 copy.39
  258.7 0.3 all_to_all.91
  259.0 0.3 copy.40
  259.3 14.9 %all_to_all.123 = bf16[32,8,1024]{2,0,1:T(8,128)(2,1)S(1)} all-to-all(bf16[32,8,1024]{2,0,1:T(8,128)(2,1)S(1)} %copy.40), channel_id=1, replica_groups=mesh['dp'=32,'tensor'=8] {'tensor'}, dimensions={1} | all-to-all | bytes 1048576 | tf_op jit(solution)/shard_map/all_to_all | solution.py:14
  274.2 1.0 fusion.21
  275.3 61.2 %all-reduce.8.cloned.1.call-done = f32[256,256]{1,0:T(8,128)} async-done(((f32[256,256]{1,0:T(8,128)}), f32[256,256]{1,0:T(8,128)}) %all-reduce.8.cloned.1.call-update) | async-done | bytes 262160 | tf_op jit(solution)/shard_map/psum | solution.py:93
  336.5 0.8 bitcast_dynamic-update-slice_fusion.2
  337.2 0.1 stack.26
  337.3 23.4 %all_to_all.124 = bf16[32,32,256]{2,1,0:T(8,128)(2,1)S(1)} all-to-all(bf16[32,32,256]{2,1,0:T(8,128)(2,1)S(1)} %stack.26), channel_id=1, replica_groups=mesh['dp'=32,'tensor'=8] {'dp'}, dimensions={0} | all-to-all | bytes 1048576 | tf_op jit(solution)/shard_map/all_to_all | solution.py:12
  360.7 0.3 copy.41
  361.0 0.3 all_to_all.96
  361.4 0.3 copy.42
  361.7 14.9 %all_to_all.125 = bf16[32,8,1024]{2,0,1:T(8,128)(2,1)S(1)} all-to-all(bf16[32,8,1024]{2,0,1:T(8,128)(2,1)S(1)} %copy.42), channel_id=1, replica_groups=mesh['dp'=32,'tensor'=8] {'tensor'}, dimensions={1} | all-to-all | bytes 1048576 | tf_op jit(solution)/shard_map/all_to_all | solution.py:14
  376.6 1.0 fusion.22
  377.7 61.2 %all-reduce.10.cloned.1.call-done = f32[256,256]{1,0:T(8,128)} async-done(((f32[256,256]{1,0:T(8,128)}), f32[256,256]{1,0:T(8,128)}) %all-reduce.10.cloned.1.call-update) | async-done | bytes 262160 | tf_op jit(solution)/shard_map/psum | solution.py:93
  438.8 0.8 bitcast_dynamic-update-slice_fusion.1
  439.6 0.1 stack.28
  439.6 23.4 %all_to_all.126 = bf16[32,32,256]{2,1,0:T(8,128)(2,1)S(1)} all-to-all(bf16[32,32,256]{2,1,0:T(8,128)(2,1)S(1)} %stack.28), channel_id=1, replica_groups=mesh['dp'=32,'tensor'=8] {'dp'}, dimensions={0} | all-to-all | bytes 1048576 | tf_op jit(solution)/shard_map/all_to_all | solution.py:12
  463.1 0.3 copy.43
  463.4 0.3 all_to_all.101
  463.7 0.3 copy.44
  464.0 14.9 %all_to_all.127 = bf16[32,8,1024]{2,0,1:T(8,128)(2,1)S(1)} all-to-all(bf16[32,8,1024]{2,0,1:T(8,128)(2,1)S(1)} %copy.44), channel_id=1, replica_groups=mesh['dp'=32,'tensor'=8] {'tensor'}, dimensions={1} | all-to-all | bytes 1048576 | tf_op jit(solution)/shard_map/all_to_all | solution.py:14
  478.9 1.0 fusion.23
  480.0 0.0 all-reduce.14.cloned.1.call-start
  480.0 61.2 %all-reduce.12.cloned.1.call-done = f32[256,256]{1,0:T(8,128)} async-done(((f32[256,256]{1,0:T(8,128)}), f32[256,256]{1,0:T(8,128)}) %all-reduce.12.cloned.1.call-update) | async-done | bytes 262160 | tf_op jit(solution)/shard_map/psum | solution.py:93
  541.2 0.8 bitcast_dynamic-update-slice_fusion
  541.9 0.1 stack.30
  542.0 23.4 %all_to_all.128 = bf16[32,32,256]{2,1,0:T(8,128)(2,1)S(1)} all-to-all(bf16[32,32,256]{2,1,0:T(8,128)(2,1)S(1)} %stack.30), channel_id=1, replica_groups=mesh['dp'=32,'tensor'=8] {'dp'}, dimensions={0} | all-to-all | bytes 1048576 | tf_op jit(solution)/shard_map/all_to_all | solution.py:12
  565.4 0.3 copy.45
  565.7 0.3 all_to_all.106
  566.1 0.3 copy.46
  566.4 14.9 %all_to_all.129 = bf16[32,8,1024]{2,0,1:T(8,128)(2,1)S(1)} all-to-all(bf16[32,8,1024]{2,0,1:T(8,128)(2,1)S(1)} %copy.46), channel_id=1, replica_groups=mesh['dp'=32,'tensor'=8] {'tensor'}, dimensions={1} | all-to-all | bytes 1048576 | tf_op jit(solution)/shard_map/all_to_all | solution.py:14
  581.3 1.0 fusion.24
  582.3 0.7 copy.47
  583.0 60.5 %all-reduce.14.cloned.1.call-done = f32[256,256]{1,0:T(8,128)} async-done(((f32[256,256]{1,0:T(8,128)}), f32[256,256]{1,0:T(8,128)}) %all-reduce.14.cloned.1.call-update) | async-done | bytes 262160 | tf_op jit(solution)/shard_map/psum | solution.py:93
  643.5 0.8 fusion.14
  644.3 0.6 copy-done.4
  (28 shorter events, 0.4 us)
Async XLA Ops:
  7.2 87.5 %copy-start = (bf16[1024,256]{1,0:T(8,128)(2,1)S(1)}, bf16[1024,256]{1,0:T(8,128)(2,1)}, u32[]{:S(2)}) copy-start(bf16[1024,256]{1,0:T(8,128)(2,1)} %param.18) | copy-start | bytes 1572868
  7.2 4.8 copy-start.2
  7.2 87.5 %all-gather.2.cloned.1.call-start = ((), (), s32[]{:S(2)}) async-start(), calls=%async_computation.11 | async-start | bytes 3244032 | tf_op jit(solution)/shard_map/all_gather | solution.py:70
  12.9 85.8 %copy-start.3 = (bf16[32,6,256]{2,0,1:T(8,128)(2,1)S(1)}, bf16[32,6,256]{2,0,1:T(8,128)(2,1)}, u32[]{:S(2)}) copy-start(bf16[32,6,256]{2,0,1:T(8,128)(2,1)} %param.17) | copy-start | bytes 294916
  12.9 85.9 %copy-start.5 = (s32[32]{0:T(128)S(1)}, s32[32]{0:T(128)}, u32[]{:S(2)}) copy-start(s32[32]{0:T(128)} %param.16) | copy-start | bytes 388
  12.9 119.0 %reduce-scatter.2.cloned.1.call-start = ((), (), s32[]{:S(2)}) async-start(), calls=%async_computation.12 | async-start | bytes 1769472 | tf_op jit(solution)/shard_map/reduce_scatter | solution.py:74
  98.7 135.4 %all-reduce.6.cloned.1.call-start = ((), (), s32[]{:S(2)}) async-start(), calls=%async_computation.13 | async-start | bytes 524288 | tf_op jit(solution)/shard_map/psum | solution.py:93
  132.8 38.0 %copy-start.1 = (bf16[1024,256]{1,0:T(8,128)(2,1)S(1)}, bf16[1024,256]{1,0:T(8,128)(2,1)}, u32[]{:S(2)}) copy-start(bf16[1024,256]{1,0:T(8,128)(2,1)} %param.19) | copy-start | bytes 1572868
  171.9 164.6 %all-reduce.8.cloned.1.call-start = ((), (), s32[]{:S(2)}) async-start(), calls=%async_computation.14 | async-start | bytes 524288 | tf_op jit(solution)/shard_map/psum | solution.py:93
  275.3 163.6 %all-reduce.10.cloned.1.call-start = ((), (), s32[]{:S(2)}) async-start(), calls=%async_computation.15 | async-start | bytes 524288 | tf_op jit(solution)/shard_map/psum | solution.py:93
  377.6 163.6 %all-reduce.12.cloned.1.call-start = ((), (), s32[]{:S(2)}) async-start(), calls=%async_computation.16 | async-start | bytes 524288 | tf_op jit(solution)/shard_map/psum | solution.py:93
  480.0 163.6 %all-reduce.14.cloned.1.call-start = ((), (), s32[]{:S(2)}) async-start(), calls=%async_computation.17 | async-start | bytes 524288 | tf_op jit(solution)/shard_map/psum | solution.py:93
  644.3 0.6 copy-start.4
Sparse Core Ops, SparseCore 0:
  13.0 81.5 all-gather.1
  98.8 33.0 reduce-scatter.1
  172.0 62.0 all-reduce.5
  275.4 61.0 all-reduce.7
  377.7 61.0 all-reduce.9
  480.1 61.0 all-reduce.11
  582.4 61.0 all-reduce.13
